TPU v7x, 256 devices: a whole 4x4x8 slice. The times are simulated.
256 devices in a mesh: dp: 64 (over z_lo, y, x, core), ckpt: 4 (over z_hi).
Axes of the slice: x: 4, y: 4, z: 8 (z_hi: 4, z_lo: 2; z = z_hi * 2 + z_lo), core: 2. Of those that a mesh axis runs over, the one named last changes fastest.
Arguments:
- layer_input: bfloat16 [32768, 6144], P(('dp', 'ckpt')), may hold values from -6 to 6
- out_grad: bfloat16 [32768, 6144], P(('dp', 'ckpt')), may hold values from -6 to 6
- router_weight: bfloat16 [32768], P(('dp', 'ckpt')), may hold values from 0.049804688 to 1
- token_slot: int32 [32768], P(('dp', 'ckpt')), may hold values from -1 to 7, as said below
- slot_token: int32 [2048], P(('dp', 'ckpt')), may hold values from -1 to 127, as said below
- gate_weight: bfloat16 [6144, 8192], P('ckpt', 'dp'), may hold values from -0.078125 to 0.078125
- up_weight: bfloat16 [6144, 8192], P('ckpt', 'dp'), may hold values from -0.078125 to 0.078125
- down_weight: bfloat16 [6144, 8192], P('ckpt', 'dp'), may hold values from -0.078125 to 0.078125
Outputs:
- input_grad: bfloat16 [32768, 6144], P(('dp', 'ckpt'))
- router_grad: float32 [32768], P(('dp', 'ckpt'))
- gate_grad: float32 [6144, 8192], P('ckpt', 'dp')
- up_grad: float32 [6144, 8192], P('ckpt', 'dp')
- down_grad: float32 [6144, 8192], P('ckpt', 'dp')
Inputs may be any that keep to these rules, and one draw needn't show every extreme that they name: `token_slot`: for each token, its row among the rows that its device sends to the expert, or -1 if the router did not send it there. A device's live rows are 0 to n - 1 for some n of 1 to 8. For each of a device's 8 rows, the index among that device's tokens of the token in it, or -1 for an empty row. Live rows come first; token_slot and slot_token are inverse to each other. In every draw all devices of some group along ckpt fill all 8 rows.
All inputs are finite; a program needn't handle non-finite values.
Results may differ from a plain program's by a relative error of at most 0.0049.
Values may be sent and summed in bfloat16 or wider, within the bound.
A program may use at most 128 MiB of HBM per device.

v0:
```python
import jax
import jax.numpy as jnp
from jax import lax
from jax.sharding import PartitionSpec as P


def local(
    layer_input,
    out_grad,
    router_weight,
    token_slot,
    slot_token,
    gate_weight,
    up_weight,
    down_weight,
):
    members = lax.axis_size("ckpt")
    row_count = slot_token.shape[0]
    is_live = slot_token >= 0
    safe_index = jnp.maximum(slot_token, 0)
    rows_input = jnp.where(
        is_live[:, None], jnp.take(layer_input, safe_index, axis=0), jnp.zeros((), jnp.bfloat16)
    )
    rows_grad = jnp.where(
        is_live[:, None], jnp.take(out_grad, safe_index, axis=0), jnp.zeros((), jnp.bfloat16)
    )
    rows_router = jnp.where(
        is_live, jnp.take(router_weight, safe_index, axis=0), jnp.zeros((), jnp.bfloat16)
    )
    router_tile = jnp.broadcast_to(rows_router[:, None], (row_count, members))
    quarter_input, quarter_grad, quarter_router = (
        lax.all_to_all(rows_input, "ckpt", split_axis=1, concat_axis=0, tiled=True),
        lax.all_to_all(rows_grad, "ckpt", split_axis=1, concat_axis=0, tiled=True),
        lax.all_to_all(router_tile, "ckpt", split_axis=1, concat_axis=0, tiled=True),
    )
    all_input, all_grad, all_router = (
        lax.all_gather(quarter_input, "dp", axis=0, tiled=True),
        lax.all_gather(quarter_grad, "dp", axis=0, tiled=True),
        lax.all_gather(quarter_router, "dp", axis=0, tiled=True),
    )
    gate_part = jnp.dot(all_input, gate_weight, preferred_element_type=jnp.float32)
    up_part = jnp.dot(all_input, up_weight, preferred_element_type=jnp.float32)
    back_part = jnp.dot(all_grad, down_weight, preferred_element_type=jnp.float32)
    gate_pre, up_pre, act_grad = lax.psum((gate_part, up_part, back_part), "ckpt")
    sigmoid_g = jax.nn.sigmoid(gate_pre)
    active = sigmoid_g * gate_pre * up_pre
    router_f = all_router.astype(jnp.float32)
    scaled = (router_f * active).astype(jnp.bfloat16)
    router_part = jnp.sum(active * act_grad, axis=1)
    act_delta = router_f * act_grad
    gate_delta = (act_delta * up_pre * sigmoid_g * (1.0 + gate_pre * (1.0 - sigmoid_g))).astype(
        jnp.bfloat16
    )
    up_delta = (act_delta * sigmoid_g * gate_pre).astype(jnp.bfloat16)
    input_part = jnp.einsum(
        "rh,dh->rd", gate_delta, gate_weight, preferred_element_type=jnp.float32
    )
    input_part = input_part + jnp.einsum(
        "rh,dh->rd", up_delta, up_weight, preferred_element_type=jnp.float32
    )
    input_sums, router_sums = (
        lax.psum_scatter(input_part, "dp", scatter_dimension=0, tiled=True),
        lax.psum_scatter(router_part, "dp", scatter_dimension=0, tiled=True),
    )
    input_quarters = input_sums.astype(jnp.bfloat16)
    input_rows = lax.all_to_all(input_quarters, "ckpt", split_axis=0, concat_axis=1, tiled=True)
    own_router = lax.dynamic_slice_in_dim(
        router_sums, lax.axis_index("ckpt") * row_count, row_count, 0
    )
    has_row = token_slot >= 0
    token_index = jnp.maximum(token_slot, 0)
    input_grad = jnp.where(
        has_row[:, None], jnp.take(input_rows, token_index, axis=0), jnp.zeros((), jnp.bfloat16)
    )
    router_grad = jnp.where(
        has_row, jnp.take(own_router, token_index, axis=0), jnp.zeros((), jnp.float32)
    )
    gate_grad = jnp.einsum("rd,rh->dh", all_input, gate_delta, preferred_element_type=jnp.float32)
    up_grad = jnp.einsum("rd,rh->dh", all_input, up_delta, preferred_element_type=jnp.float32)
    down_grad = jnp.einsum("rd,rh->dh", all_grad, scaled, preferred_element_type=jnp.float32)
    return (input_grad, router_grad, gate_grad, up_grad, down_grad)


def solution(mesh):
    return jax.shard_map(
        local,
        mesh=mesh,
        in_specs=(
            P(("dp", "ckpt"), None),
            P(("dp", "ckpt"), None),
            P(("dp", "ckpt")),
            P(("dp", "ckpt")),
            P(("dp", "ckpt")),
            P("ckpt", "dp"),
            P("ckpt", "dp"),
            P("ckpt", "dp"),
        ),
        out_specs=(
            P(("dp", "ckpt"), None),
            P(("dp", "ckpt")),
            P("ckpt", "dp"),
            P("ckpt", "dp"),
            P("ckpt", "dp"),
        ),
        check_vma=False,
    )
```

profile of v0, /device:TPU:32, one launch (start us, length us, event | category | flops | bytes accessed | tf_op | source)
XLA Modules:
  0.0 764.8 jit_solution(3806657502283674632)
XLA Ops:
  7.2 0.0 copy-start
  7.2 0.0 all-gather.5.cloned.1.call-start
  7.2 0.8 broadcast_maximum_fusion
  8.0 0.7 broadcast_compare_fusion.1
  8.7 0.0 copy-done
  8.7 0.0 copy-start.4
  8.7 0.6 gather_fusion.3
  9.3 2.3 gather_fusion.2
  11.6 0.1 select_select_fusion.2
  11.7 16.1 %all_to_all.73 = bf16[8,4,1536]{2,0,1:T(8,128)(2,1)} all-to-all(bf16[8,4,1536]{2,0,1:T(8,128)(2,1)S(1)} %bitcast.46), channel_id=1, replica_groups=mesh['dp'=64,'ckpt'=4] {'ckpt'}, dimensions={1} | all-to-all | bytes 196608 | tf_op jit(solution)/shard_map/all_to_all | solution.py:32
  27.8 0.0 all-gather.5.cloned.1.call-update
  27.8 0.0 all-gather.3.cloned.1.call-start
  27.9 11.5 %all_to_all.74 = bf16[8,4,1536]{2,0,1:T(8,128)(2,1)} all-to-all(bf16[8,4,1536]{2,0,1:T(8,128)(2,1)S(1)} %bitcast.45), channel_id=1, replica_groups=mesh['dp'=64,'ckpt'=4] {'ckpt'}, dimensions={1} | all-to-all | bytes 196608 | tf_op jit(solution)/shard_map/all_to_all | solution.py:33
  39.4 0.0 all-gather.3.cloned.1.call-update
  39.4 0.0 all-reduce.5.cloned.1.call-start
  39.5 95.5 %all-gather.5.cloned.1.call-done = bf16[2048,1536]{1,0:T(8,128)(2,1)} async-done(((bf16[32,1536]{1,0:T(8,128)(2,1)}), bf16[2048,1536]{1,0:T(8,128)(2,1)}) %all-gather.5.cloned.1.call-update) | async-done | bytes 6291472 | tf_op jit(solution)/shard_map/all_gather | solution.py:37
  134.9 0.0 copy-start.2
  134.9 5.7 fusion.8
  140.7 0.0 copy-done.4
  140.7 0.0 copy-done.2
  140.7 0.0 copy-start.7
  140.7 2.8 fusion.7
  143.5 0.0 copy-start.1
  143.5 0.0 copy-start.8
  143.5 102.3 %all-gather.3.cloned.1.call-done = bf16[2048,1536]{1,0:T(8,128)(2,1)} async-done(((bf16[32,1536]{1,0:T(8,128)(2,1)}), bf16[2048,1536]{1,0:T(8,128)(2,1)}) %all-gather.3.cloned.1.call-update) | async-done | bytes 6291472 | tf_op jit(solution)/shard_map/all_gather | solution.py:38
  245.8 0.0 copy-done.7
  245.8 5.6 fusion.6
  251.4 0.0 all-reduce.5.cloned.1.call-update
  251.4 0.0 copy-done.1
  251.4 0.6 gather_fusion
  252.1 0.0 copy-done.10
  252.1 0.6 broadcast_in_dim.80
  252.7 6.4 all-to-all-start
  259.1 0.0 reduce-scatter.2.cloned.1.call-start
  259.1 0.0 copy-done.8
  259.1 0.6 fusion.4
  260.4 6.4 all-to-all-done
  266.8 0.1 reshape.97
  266.9 0.2 dynamic-update-slice
  267.1 153.7 %all-reduce = bf16[2048]{0:T(1024)(128)(2,1)S(1)} all-reduce(bf16[2048]{0:T(1024)(128)(2,1)S(1)} %dynamic-update-slice), channel_id=1, replica_groups=mesh['dp'=64,'ckpt'=4] {'dp'}, use_global_device_ids=true, to_apply=%add | all-reduce | flops 2048 | bytes 8192
  420.8 0.0 all-reduce.5.cloned.1.call-done
  420.8 2.7 multiply_reduce_fusion
  423.6 0.0 copy-done.3
  423.6 1.8 fusion.9
  425.4 6.4 convolution_add_fusion
  431.8 0.0 reduce-scatter.2.cloned.1.call-update
  432.5 0.0 copy-done.9
  432.5 141.2 %all-reduce.1 = f32[2048]{0:T(1024)S(1)} all-reduce(f32[2048]{0:T(1024)S(1)} %get-tuple-element.9), channel_id=3, replica_groups=mesh['dp'=64,'ckpt'=4] {'dp'}, use_global_device_ids=true, to_apply=%region_5.7.clone | all-reduce | flops 2048 | bytes 16384
  573.7 0.1 dynamic_slice.3
  573.8 0.7 fusion.5
  574.5 5.7 fusion.10
  580.2 5.7 fusion.11
  585.9 0.0 slice-done
  585.9 0.0 copy-done.5
  585.9 0.0 copy-done.6
  585.9 0.0 slice-done.1
  585.9 3.1 fusion
  589.0 149.7 %reduce-scatter.2.cloned.1.call-done = f32[32,1536]{1,0:T(8,128)} async-done(((f32[2048,1536]{1,0:T(8,128)}), f32[32,1536]{1,0:T(8,128)}) %reduce-scatter.2.cloned.1.call-update) | async-done | bytes 196624 | tf_op jit(solution)/shard_map/reduce_scatter | solution.py:62
  738.8 1.6 convert_bitcast_fusion
  740.3 6.4 all-to-all-start.3
  746.7 5.6 fusion.3
  752.3 3.1 all-to-all-done.3
  755.4 1.5 gather_fusion.1
  756.9 1.4 select_select_fusion
  (16 shorter events, 0.1 us)
Async XLA Ops:
  7.2 1.5 copy-start
  7.2 127.7 %all-gather.5.cloned.1.call-start = ((), (), s32[]{:S(2)}) async-start(), calls=%async_computation.6 | async-start | bytes 6389760 | tf_op jit(solution)/shard_map/all_gather | solution.py:37
  8.7 132.0 %copy-start.4 = (bf16[1536,128]{1,0:T(8,128)(2,1)S(1)}, bf16[1536,128]{1,0:T(8,128)(2,1)}, u32[]{:S(2)}) copy-start(bf16[1536,128]{1,0:T(8,128)(2,1)} %param.16) | copy-start | bytes 1179652
  27.8 218.0 %all-gather.3.cloned.1.call-start = ((), (), s32[]{:S(2)}) async-start(), calls=%async_computation.5 | async-start | bytes 6389760 | tf_op jit(solution)/shard_map/all_gather | solution.py:38
  39.4 381.4 %all-reduce.5.cloned.1.call-start = ((), (), s32[]{:S(2)}) async-start(), calls=%async_computation.8 | async-start | bytes 6291456 | tf_op jit(solution)/shard_map/psum | solution.py:44
  134.9 5.7 copy-start.2
  140.7 105.2 %copy-start.7 = (bf16[1536,128]{1,0:T(8,128)(2,1)S(1)}, bf16[1536,128]{1,0:T(8,128)(2,1)}, u32[]{:S(2)}) copy-start(bf16[1536,128]{1,0:T(8,128)(2,1)} %param.17) | copy-start | bytes 1179652
  143.5 107.9 %copy-start.1 = (bf16[128]{0:T(256)(128)(2,1)S(1)}, bf16[128]{0:T(256)(128)(2,1)}, u32[]{:S(2)}) copy-start(bf16[128]{0:T(256)(128)(2,1)} %param.12) | copy-start | bytes 772
  143.5 108.5 %copy-start.10 = (s32[8]{0:T(128)S(1)}, s32[8]{0:T(128)}, u32[]{:S(2)}) copy-start(s32[8]{0:T(128)} %param.14) | copy-start | bytes 100
  143.5 115.6 %copy-start.8 = (u32[256]{0:T(256)S(1)}, u32[256]{0:T(256)}, u32[]{:S(2)}) copy-start(u32[256]{0:T(256)} %constant.88) | copy-start | bytes 3076
  251.4 172.2 %copy-start.3 = (bf16[1536,128]{1,0:T(8,128)(2,1)S(1)}, bf16[1536,128]{1,0:T(8,128)(2,1)}, u32[]{:S(2)}) copy-start(bf16[1536,128]{1,0:T(8,128)(2,1)} %param.15) | copy-start | bytes 1179652
  252.7 14.1 %all-to-all-start = ((bf16[8,4,1]{0,2,1:T(2,128)(2,1)}), bf16[8,4,1]{0,2,1:T(2,128)(2,1)S(1)}, u32[]{:S(2)}, u32[]{:S(2)}) async-start(bf16[8,4,1]{0,2,1:T(2,128)(2,1)} %broadcast_in_dim.80), calls=%async_computation | async-start | bytes 4096 | tf_op jit(solution)/shard_map/all_to_all | solution.py:34
  259.1 479.6 %reduce-scatter.2.cloned.1.call-start = ((), (), s32[]{:S(2)}) async-start(), calls=%async_computation.7 | async-start | bytes 12779520 | tf_op jit(solution)/shard_map/reduce_scatter | solution.py:62
  431.8 0.7 copy-start.9
  574.5 11.4 %slice-start = ((s8[6291456]{0:T(1024)(128)(4,1)}), s8[4194304]{0:T(1024)(128)(4,1)S(1)}, s32[]{:S(2)}) async-start(s8[6291456]{0:T(1024)(128)(4,1)} %bitcast.41), calls=%async_computation.9 | async-start | bytes 8388608
  574.5 11.4 %copy-start.5 = (f32[2048,128]{1,0:T(8,128)S(1)}, f32[2048,128]{1,0:T(8,128)}, u32[]{:S(2)}) copy-start(f32[2048,128]{1,0:T(8,128)} %get-tuple-element.6) | copy-start | bytes 3145732
  574.5 11.4 %copy-start.6 = (f32[2048,128]{1,0:T(8,128)S(1)}, f32[2048,128]{1,0:T(8,128)}, u32[]{:S(2)}) copy-start(f32[2048,128]{1,0:T(8,128)} %get-tuple-element.7) | copy-start | bytes 3145732
  580.2 5.7 slice-start.1
  740.3 15.1 %all-to-all-start.3 = ((bf16[4,8,1536]{2,1,0:T(8,128)(2,1)}), bf16[4,8,1536]{2,1,0:T(8,128)(2,1)S(1)}, u32[]{:S(2)}, u32[]{:S(2)}) async-start(bf16[4,8,1536]{2,1,0:T(8,128)(2,1)} %convert_bitcast_fusion), calls=%async_computation.4 | async-start | bytes 196608 | tf_op jit(solution)/shard_map/all_to_all | solution.py:66
Sparse Core Ops, SparseCore 0:
  27.9 106.9 all-gather.4
  136.8 108.9 all-gather.2
  251.5 131.6 all-reduce.4
  431.9 306.7 reduce-scatter.1
where the time goes:
time: 765 us
  waiting for transfers between devices  357 us (47%)
  blocking collectives  322 us (42%)
  matrix products  36.8 us (5%)
  between operations  15.2 us (2%)
  starting transfers between devices  12.9 us (2%)
  other arithmetic  12.8 us (2%)
    unnamed x2, blocking collectives  295 us
    reduce_scatter x1, waiting for transfers between devices, local(): lax.psum_scatter(input_part, 'dp', scatter_dimension=0, tiled=True)  150 us
    all_gather x1, waiting for transfers between devices, local(): lax.all_gather(quarter_grad, 'dp', axis=0, tiled=True)  102 us
    all_gather x1, waiting for transfers between devices, local(): lax.all_gather(quarter_input, 'dp', axis=0, tiled=True)  95.5 us
    all_to_all x1, blocking collectives, local(): lax.all_to_all(rows_input, 'ckpt', split_axis=1, concat_axis=0, tiled=True)  16.1 us
  transfers between devices with their start and end apart: 6, of which 5 were waited for; matrix products, arithmetic and copies ran while one was open for 4% of the time, Pallas kernels for 0%

commit v1 on v0

--- a/solution.py
+++ b/solution.py
@@ -2,6 +2,14 @@
 import jax.numpy as jnp
 from jax import lax
 from jax.sharding import PartitionSpec as P
+
+
+def _touch_pairs_all(named_axis, field_in):
+    piece_next = lax.axis_size(named_axis)
+    s_next = jnp.stack(piece_next * [field_in])
+    odd = lax.all_to_all(s_next, axis_name=named_axis, split_axis=0, concat_axis=0)
+    even = jnp.concatenate(odd, 0)
+    return even
 
 
 def local(
@@ -34,7 +42,7 @@
         lax.all_to_all(router_tile, "ckpt", split_axis=1, concat_axis=0, tiled=True),
     )
     all_input, all_grad, all_router = (
-        lax.all_gather(quarter_input, "dp", axis=0, tiled=True),
+        _touch_pairs_all("dp", quarter_input),
         lax.all_gather(quarter_grad, "dp", axis=0, tiled=True),
         lax.all_gather(quarter_router, "dp", axis=0, tiled=True),
     )

time: 765 us -> 736 us (0.962)
  waiting for transfers between devices: 357 us -> 314 us
    all_gather x1 -> x0, waiting for transfers between devices: 95.5 us -> none  [local(): lax.all_gather(quarter_input, 'dp', axis=0, tiled=True)]
    all_to_all x0 -> x1, waiting for transfers between devices: none -> 78.6 us  [_touch_pairs_all(): lax.all_to_all(s_next, axis_name=named_axis, split_axis=0, concat_axis=0)]
    all_gather x1, waiting for transfers between devices: 102 us -> 75.3 us  [local(): lax.all_gather(quarter_grad, 'dp', axis=0, tiled=True)]
    all_to_all x0 -> x1, starting transfers between devices: none -> 9.35 us  [_touch_pairs_all(): lax.all_to_all(s_next, axis_name=named_axis, split_axis=0, concat_axis=0)]
  transfers between devices with their start and end apart: 6 -> 6, of which waited for: 5 -> 5; matrix products, arithmetic and copies ran while one was open for 4% -> 5% of each run, Pallas kernels for 0% -> 0%
where the time goes in v1:
time: 736 us; the launch traced here: 735 us
  blocking collectives  323 us (44%)
  waiting for transfers between devices  314 us (43%)
  matrix products  39.4 us (5%)
  starting transfers between devices  19.8 us (3%)
  between operations  15.3 us (2%)
  other arithmetic  12.7 us (2%)
  local copies, waits for them, and re-layouts  10.8 us (1%)
    unnamed x2, blocking collectives  295 us
    reduce_scatter x1, waiting for transfers between devices, local(): lax.psum_scatter(input_part, 'dp', scatter_dimension=0, tiled=True)  150 us
    all_to_all x1, waiting for transfers between devices, _touch_pairs_all(): lax.all_to_all(s_next, axis_name=named_axis, split_axis=0, concat_axis=0)  78.6 us
    all_gather x1, waiting for transfers between devices, local(): lax.all_gather(quarter_grad, 'dp', axis=0, tiled=True)  75.3 us
    all_to_all x1, blocking collectives, local(): lax.all_to_all(rows_input, 'ckpt', split_axis=1, concat_axis=0, tiled=True)  16 us
  transfers between devices with their start and end apart: 6, of which 5 were waited for; matrix products, arithmetic and copies ran while one was open for 5% of the time, Pallas kernels for 0%

profile of v1, /device:TPU:32, one launch (start us, length us, event | category | flops | bytes accessed | tf_op | source)
XLA Modules:
  0.0 735.0 jit_solution(8124611549551368379)
XLA Ops:
  7.2 0.0 copy-start
  7.2 0.8 broadcast_maximum_fusion
  8.0 0.7 broadcast_compare_fusion.1
  8.6 0.0 copy-done
  8.6 0.6 gather_fusion.3
  9.2 2.3 gather_fusion.2
  11.6 0.1 select_select_fusion.2
  11.7 16.0 %all_to_all.75 = bf16[8,4,1536]{2,0,1:T(8,128)(2,1)S(1)} all-to-all(bf16[8,4,1536]{2,0,1:T(8,128)(2,1)S(1)} %bitcast.46), channel_id=1, replica_groups=mesh['dp'=64,'ckpt'=4] {'ckpt'}, dimensions={1} | all-to-all | bytes 196608 | tf_op jit(solution)/shard_map/all_to_all | solution.py:40
  27.6 11.5 %all_to_all.76 = bf16[8,4,1536]{2,0,1:T(8,128)(2,1)} all-to-all(bf16[8,4,1536]{2,0,1:T(8,128)(2,1)S(1)} %bitcast.45), channel_id=1, replica_groups=mesh['dp'=64,'ckpt'=4] {'ckpt'}, dimensions={1} | all-to-all | bytes 196608 | tf_op jit(solution)/shard_map/all_to_all | solution.py:41
  39.1 3.4 stack.5
  42.6 0.0 copy-start.2
  42.6 9.3 %all-to-all-start.3 = ((bf16[64,32,1536]{2,1,0:T(8,128)(2,1)}), bf16[64,32,1536]{2,1,0:T(8,128)(2,1)}, u32[]{:S(2)}, u32[]{:S(2)}) async-start(bf16[64,32,1536]{2,1,0:T(8,128)(2,1)} %stack.5), calls=%async_computation.3 | async-start | bytes 12582912 | tf_op jit(solution)/shard_map/all_to_all | solution.py:10
  51.9 0.0 copy-start.3
  51.9 0.0 all-gather.2.cloned.1.call-start
  52.0 0.7 all-gather.2.cloned.1.call-update
  52.7 0.0 all-reduce.5.cloned.1.call-start
  52.7 78.6 %all-to-all-done.3 = bf16[64,32,1536]{2,1,0:T(8,128)(2,1)} async-done(((bf16[64,32,1536]{2,1,0:T(8,128)(2,1)}), bf16[64,32,1536]{2,1,0:T(8,128)(2,1)}, u32[]{:S(2)}, u32[]{:S(2)}) %all-to-all-start.3) | async-done | bytes 6291488 | tf_op jit(solution)/shard_map/all_to_all | solution.py:10
  131.3 0.0 copy-done.2
  131.3 5.5 fusion.8
  136.9 0.0 copy-done.3
  136.9 0.0 copy-start.6
  136.9 5.6 fusion.7
  142.5 0.0 copy-start.1
  142.5 0.0 copy-start.9
  142.5 75.3 %all-gather.2.cloned.1.call-done = bf16[2048,1536]{1,0:T(8,128)(2,1)} async-done(((bf16[32,1536]{1,0:T(8,128)(2,1)}), bf16[2048,1536]{1,0:T(8,128)(2,1)}) %all-gather.2.cloned.1.call-update) | async-done | bytes 6291472 | tf_op jit(solution)/shard_map/all_gather | solution.py:46
  217.8 0.0 copy-done.6
  217.8 5.5 fusion.6
  223.4 0.0 all-reduce.5.cloned.1.call-update
  223.4 0.0 copy-done.1
  223.4 0.6 gather_fusion
  224.1 0.0 copy-done.9
  224.1 0.6 broadcast_in_dim.80
  224.7 3.2 all-to-all-start
  227.9 0.0 reduce-scatter.2.cloned.1.call-start
  228.0 0.0 copy-done.7
  228.0 0.6 fusion.4
  229.2 6.3 all-to-all-done
  235.6 0.1 reshape.104
  235.6 0.2 dynamic-update-slice
  235.8 153.9 %all-reduce = bf16[2048]{0:T(1024)(128)(2,1)S(1)} all-reduce(bf16[2048]{0:T(1024)(128)(2,1)S(1)} %dynamic-update-slice), channel_id=1, replica_groups=mesh['dp'=64,'ckpt'=4] {'dp'}, use_global_device_ids=true, to_apply=%add | all-reduce | flops 2048 | bytes 8192
  389.7 0.0 all-reduce.5.cloned.1.call-done
  389.7 2.7 multiply_reduce_fusion
  392.5 1.8 fusion.9
  394.3 6.4 convolution_add_fusion
  400.7 0.0 reduce-scatter.2.cloned.1.call-update
  401.4 0.0 copy-done.8
  401.4 141.3 %all-reduce.1 = f32[2048]{0:T(1024)S(1)} all-reduce(f32[2048]{0:T(1024)S(1)} %get-tuple-element.9), channel_id=3, replica_groups=mesh['dp'=64,'ckpt'=4] {'dp'}, use_global_device_ids=true, to_apply=%region_5.7.clone | all-reduce | flops 2048 | bytes 16384
  542.7 0.1 dynamic_slice.3
  542.8 0.7 fusion.5
  543.4 0.0 copy-start.5
  543.4 5.7 fusion.10
  549.1 5.7 fusion.11
  554.8 0.0 slice-done
  554.8 0.0 copy-done.4
  554.8 0.0 copy-done.5
  554.8 0.0 slice-done.1
  554.8 3.1 fusion
  558.0 150.5 %reduce-scatter.2.cloned.1.call-done = f32[32,1536]{1,0:T(8,128)} async-done(((f32[2048,1536]{1,0:T(8,128)}), f32[32,1536]{1,0:T(8,128)}) %reduce-scatter.2.cloned.1.call-update) | async-done | bytes 196624 | tf_op jit(solution)/shard_map/reduce_scatter | solution.py:70
  708.4 1.6 convert_bitcast_fusion
  710.0 7.1 all-to-all-start.4
  717.1 5.4 fusion.3
  722.5 3.0 all-to-all-done.4
  725.6 1.5 gather_fusion.1
  727.1 1.4 select_select_fusion
  (14 shorter events, 0.1 us)
Async XLA Ops:
  7.2 1.5 copy-start
  42.6 88.8 %copy-start.2 = (bf16[1536,128]{1,0:T(8,128)(2,1)S(1)}, bf16[1536,128]{1,0:T(8,128)(2,1)}, u32[]{:S(2)}) copy-start(bf16[1536,128]{1,0:T(8,128)(2,1)} %param.15) | copy-start | bytes 1179652
  42.6 88.8 %all-to-all-start.3 = ((bf16[64,32,1536]{2,1,0:T(8,128)(2,1)}), bf16[64,32,1536]{2,1,0:T(8,128)(2,1)}, u32[]{:S(2)}, u32[]{:S(2)}) async-start(bf16[64,32,1536]{2,1,0:T(8,128)(2,1)} %stack.5), calls=%async_computation.3 | async-start | bytes 12582912 | tf_op jit(solution)/shard_map/all_to_all | solution.py:10
  51.9 85.0 %copy-start.3 = (bf16[1536,128]{1,0:T(8,128)(2,1)S(1)}, bf16[1536,128]{1,0:T(8,128)(2,1)}, u32[]{:S(2)}) copy-start(bf16[1536,128]{1,0:T(8,128)(2,1)} %param.16) | copy-start | bytes 1179652
  51.9 165.9 %all-gather.2.cloned.1.call-start = ((), (), s32[]{:S(2)}) async-start(), calls=%async_computation.6 | async-start | bytes 6389760 | tf_op jit(solution)/shard_map/all_gather | solution.py:46
  52.7 337.1 %all-reduce.5.cloned.1.call-start = ((), (), s32[]{:S(2)}) async-start(), calls=%async_computation.8 | async-start | bytes 6291456 | tf_op jit(solution)/shard_map/psum | solution.py:52
  136.9 80.9 %copy-start.6 = (bf16[1536,128]{1,0:T(8,128)(2,1)S(1)}, bf16[1536,128]{1,0:T(8,128)(2,1)}, u32[]{:S(2)}) copy-start(bf16[1536,128]{1,0:T(8,128)(2,1)} %param.17) | copy-start | bytes 1179652
  142.5 80.9 %copy-start.1 = (bf16[128]{0:T(256)(128)(2,1)S(1)}, bf16[128]{0:T(256)(128)(2,1)}, u32[]{:S(2)}) copy-start(bf16[128]{0:T(256)(128)(2,1)} %param.12) | copy-start | bytes 772
  142.5 81.5 %copy-start.9 = (s32[8]{0:T(128)S(1)}, s32[8]{0:T(128)}, u32[]{:S(2)}) copy-start(s32[8]{0:T(128)} %param.14) | copy-start | bytes 100
  142.5 85.4 %copy-start.7 = (u32[256]{0:T(256)S(1)}, u32[256]{0:T(256)}, u32[]{:S(2)}) copy-start(u32[256]{0:T(256)} %constant.88) | copy-start | bytes 3076
  224.7 10.9 %all-to-all-start = ((bf16[8,4,1]{0,2,1:T(2,128)(2,1)}), bf16[8,4,1]{0,2,1:T(2,128)(2,1)S(1)}, u32[]{:S(2)}, u32[]{:S(2)}) async-start(bf16[8,4,1]{0,2,1:T(2,128)(2,1)} %broadcast_in_dim.80), calls=%async_computation | async-start | bytes 4096 | tf_op jit(solution)/shard_map/all_to_all | solution.py:42
  227.9 480.5 %reduce-scatter.2.cloned.1.call-start = ((), (), s32[]{:S(2)}) async-start(), calls=%async_computation.7 | async-start | bytes 12779520 | tf_op jit(solution)/shard_map/reduce_scatter | solution.py:70
  400.7 0.7 copy-start.8
  543.4 11.4 %slice-start = ((s8[6291456]{0:T(1024)(128)(4,1)}), s8[4194304]{0:T(1024)(128)(4,1)S(1)}, s32[]{:S(2)}) async-start(s8[6291456]{0:T(1024)(128)(4,1)} %bitcast.42), calls=%async_computation.9 | async-start | bytes 8388608
  543.4 11.4 %copy-start.4 = (f32[2048,128]{1,0:T(8,128)S(1)}, f32[2048,128]{1,0:T(8,128)}, u32[]{:S(2)}) copy-start(f32[2048,128]{1,0:T(8,128)} %get-tuple-element.6) | copy-start | bytes 3145732
  543.4 11.4 %copy-start.5 = (f32[2048,128]{1,0:T(8,128)S(1)}, f32[2048,128]{1,0:T(8,128)}, u32[]{:S(2)}) copy-start(f32[2048,128]{1,0:T(8,128)} %get-tuple-element.7) | copy-start | bytes 3145732
  549.1 5.7 slice-start.1
  710.0 15.6 %all-to-all-start.4 = ((bf16[4,8,1536]{2,1,0:T(8,128)(2,1)}), bf16[4,8,1536]{2,1,0:T(8,128)(2,1)S(1)}, u32[]{:S(2)}, u32[]{:S(2)}) async-start(bf16[4,8,1536]{2,1,0:T(8,128)(2,1)} %convert_bitcast_fusion), calls=%async_computation.5 | async-start | bytes 196608 | tf_op jit(solution)/shard_map/all_to_all | solution.py:74
Sparse Core Ops, SparseCore 0:
  54.6 163.1 all-gather.1
  223.5 128.7 all-reduce.4
  400.8 307.5 reduce-scatter.1
